TPU v7x, 32 devices: a whole 2x2x4 slice. The times are simulated.
32 devices in a mesh: nodes: 16 (over z, y, x), rep: 2 (over core).
Axes of the slice: x: 2, y: 2, z: 4, core: 2. Of those that a mesh axis runs over, the one named last changes fastest.
Arguments:
- node_latent: bfloat16 [5120, 512], P(('nodes', 'rep')), may hold values from -6 to 6
- edge_saved: bfloat16 [40960, 512], P(('nodes', 'rep')), may hold values from -6 to 6
- node_cot: bfloat16 [5120, 512], P(('nodes', 'rep')), may hold values from -6 to 6
- edge_cot: bfloat16 [40960, 512], P(('nodes', 'rep')), may hold values from -6 to 6
- senders: int32 [40960], P(('nodes', 'rep')), may hold values from 0 to 447, as said below
- receivers: int32 [40960], P(('nodes', 'rep')), may hold values from 0 to 319
- ghost_rows: int32 [16, 16, 8], P('nodes'), may hold values from 0 to 319, as said below
- w_edge_in: bfloat16 [1536, 512], replicated, may hold values from -0.15625 to 0.15625
- w_edge_out: bfloat16 [512, 512], replicated, may hold values from -0.25 to 0.25
- edge_gain: float32 [512], replicated, may hold values from 0.5 to 2
- edge_offset: float32 [512], replicated, may hold values from -3 to 3
- w_node_in: bfloat16 [1024, 512], replicated, may hold values from -0.1875 to 0.1875
- w_node_out: bfloat16 [512, 512], replicated, may hold values from -0.25 to 0.25
- node_gain: float32 [512], replicated, may hold values from 0.5 to 2
Outputs:
- grad_nodes: bfloat16 [5120, 512], P(('nodes', 'rep'))
- grad_edges: bfloat16 [40960, 512], P(('nodes', 'rep'))
- grad_edge_in: bfloat16 [1536, 512], replicated
- grad_edge_out: bfloat16 [512, 512], replicated
- grad_node_in: bfloat16 [1024, 512], replicated
- grad_node_out: bfloat16 [512, 512], replicated
Inputs may be any that keep to these rules, and one draw needn't show every extreme that they name: `senders`: A sender below 320 is a node of the edge's own partition; otherwise it is 320 + q * 8 + s, the ghost slot s of the list of a partition q other than the edge's own. Each list ghost_rows[q, p] holds 8 distinct rows.
All inputs are finite; a program needn't handle non-finite values.
Results may differ from a plain program's by a relative error of at most 0.008.
Values may be sent and summed in bfloat16 or wider, within the bound.
A program may use at most 128 MiB of HBM per device.

v0:
```python
import math
import jax
import jax.numpy as jnp
from jax import lax
from jax.sharding import PartitionSpec as P

EPS = 1e-05


def swapped(array, axis, bit):
    return lax.ppermute(array, axis, [(i, i ^ 1 << bit) for i in range(lax.axis_size(axis))])


def mat_mul(left, right):
    return jnp.dot(left, right, preferred_element_type=jnp.float32)


def mat_tn(left, right):
    return lax.dot_general(
        left, right, (((0,), (0,)), ((), ())), preferred_element_type=jnp.float32
    )


def mat_nt(left, right):
    return lax.dot_general(
        left, right, (((1,), (1,)), ((), ())), preferred_element_type=jnp.float32
    )


def silu_slope(value):
    sigmoid_v = jax.nn.sigmoid(value)
    return sigmoid_v * (1.0 + value * (1.0 - sigmoid_v))


def norm_forward(value):
    centred = value - jnp.mean(value, axis=-1, keepdims=True)
    inverse = lax.rsqrt(jnp.mean(centred * centred, axis=-1, keepdims=True) + EPS)
    return (centred * inverse, inverse)


def norm_backward(grad_hat, normed, inverse):
    return inverse * (
        grad_hat
        - jnp.mean(grad_hat, axis=-1, keepdims=True)
        - normed * jnp.mean(grad_hat * normed, axis=-1, keepdims=True)
    )


def edge_forward(edge_block, send_rows, recv_rows, w_edge_in, w_edge_out, edge_gain, edge_offset):
    latent_width = edge_block.shape[1]
    pre_act = (
        mat_mul(edge_block, w_edge_in[:latent_width])
        + mat_mul(send_rows, w_edge_in[latent_width : 2 * latent_width])
        + mat_mul(recv_rows, w_edge_in[2 * latent_width :])
    )
    edge_hidden = jax.nn.silu(pre_act).astype(jnp.bfloat16)
    edge_normed, edge_inverse = norm_forward(mat_mul(edge_hidden, w_edge_out))
    message = edge_normed * edge_gain + edge_offset
    return (pre_act, edge_hidden, edge_normed, edge_inverse, message)


def edge_backward(
    edge_block,
    send_rows,
    recv_rows,
    edge_cot,
    message_grad,
    saved,
    w_edge_in,
    w_edge_out,
    edge_gain,
):
    pre_act, edge_hidden, edge_normed, edge_inverse = saved
    latent_width = edge_block.shape[1]
    grad_out = norm_backward(message_grad * edge_gain, edge_normed, edge_inverse).astype(
        jnp.bfloat16
    )
    grad_act = (mat_nt(grad_out, w_edge_out) * silu_slope(pre_act)).astype(jnp.bfloat16)
    in_grad = jnp.concatenate(
        [mat_tn(edge_block, grad_act), mat_tn(send_rows, grad_act), mat_tn(recv_rows, grad_act)], 0
    )
    out_grad = mat_tn(edge_hidden, grad_out)
    edge_grad = (edge_cot.astype(jnp.float32) + mat_nt(grad_act, w_edge_in[:latent_width])).astype(
        jnp.bfloat16
    )
    send_grad = mat_nt(grad_act, w_edge_in[latent_width : 2 * latent_width])
    recv_grad = mat_nt(grad_act, w_edge_in[2 * latent_width :])
    return (edge_grad, send_grad, recv_grad, in_grad, out_grad)


def node_pass(node_rows, totals_b, node_cot, w_node_in, w_node_out, node_gain):
    latent_width = node_rows.shape[1]
    node_pre = mat_mul(node_rows, w_node_in[:latent_width]) + mat_mul(
        totals_b, w_node_in[latent_width:]
    )
    node_hidden = jax.nn.silu(node_pre).astype(jnp.bfloat16)
    node_normed, node_inverse = norm_forward(mat_mul(node_hidden, w_node_out))
    grad_out = norm_backward(
        node_cot.astype(jnp.float32) * node_gain, node_normed, node_inverse
    ).astype(jnp.bfloat16)
    grad_act = (mat_nt(grad_out, w_node_out) * silu_slope(node_pre)).astype(jnp.bfloat16)
    in_grad = jnp.concatenate([mat_tn(node_rows, grad_act), mat_tn(totals_b, grad_act)], 0)
    direct_grad = mat_nt(grad_act, w_node_in[:latent_width])
    totals_grad = mat_nt(grad_act, w_node_in[latent_width:]).astype(jnp.bfloat16)
    return (direct_grad, totals_grad, in_grad, mat_tn(node_hidden, grad_out))


def shards(
    node_latent,
    edge_saved,
    node_cot,
    edge_cot,
    senders,
    receivers,
    ghost_rows,
    w_edge_in,
    w_edge_out,
    edge_gain,
    edge_offset,
    w_node_in,
    w_node_out,
    node_gain,
):
    latent_width = node_latent.shape[1]
    edge_latent = swapped(edge_saved, "rep", 0)
    partition = lax.all_gather(node_latent, "rep", axis=0, tiled=True)
    part_rows = partition.shape[0]
    ghost_lists = ghost_rows[0]
    part_count = ghost_lists.shape[0]
    slot_count = ghost_lists.shape[1]
    outgoing = partition[ghost_lists.reshape(-1)].reshape(part_count, slot_count, latent_width)
    ghosts = lax.all_to_all(outgoing, "nodes", split_axis=0, concat_axis=0, tiled=True)
    node_table = jnp.concatenate(
        [partition, ghosts.reshape(part_count * slot_count, latent_width)], 0
    )
    send_rows = node_table[senders]
    recv_rows = partition[receivers]
    pre_act, edge_hidden, edge_normed, edge_inverse, message = edge_forward(
        edge_latent, send_rows, recv_rows, w_edge_in, w_edge_out, edge_gain, edge_offset
    )
    partial_totals = jax.ops.segment_sum(message, receivers, num_segments=part_rows)
    totals = lax.psum_scatter(partial_totals, "rep", scatter_dimension=0, tiled=True)
    direct_grad, totals_grad, node_in_grad, node_out_grad = node_pass(
        node_latent, totals.astype(jnp.bfloat16), node_cot, w_node_in, w_node_out, node_gain
    )
    partition_totals_grad = lax.all_gather(totals_grad, "rep", axis=0, tiled=True)
    message_grad = edge_cot.astype(jnp.float32) + partition_totals_grad[receivers].astype(
        jnp.float32
    )
    edge_grad, send_grad, recv_grad, edge_in_grad, edge_out_grad = edge_backward(
        edge_latent,
        send_rows,
        recv_rows,
        edge_cot,
        message_grad,
        (pre_act, edge_hidden, edge_normed, edge_inverse),
        w_edge_in,
        w_edge_out,
        edge_gain,
    )
    table_grad = jax.ops.segment_sum(send_grad, senders, num_segments=node_table.shape[0])
    row_grad = table_grad[:part_rows] + jax.ops.segment_sum(
        recv_grad, receivers, num_segments=part_rows
    )
    ghost_grad = table_grad[part_rows:].reshape(part_count, slot_count, latent_width)
    returned = lax.all_to_all(
        ghost_grad.astype(jnp.bfloat16), "nodes", split_axis=0, concat_axis=0, tiled=True
    ).astype(ghost_grad.dtype)
    row_grad = row_grad + jax.ops.segment_sum(
        returned.reshape(-1, latent_width), ghost_lists.reshape(-1), num_segments=part_rows
    )
    own_grad = lax.psum_scatter(row_grad, "rep", scatter_dimension=0, tiled=True)
    grad_nodes = (own_grad + direct_grad + node_cot.astype(jnp.float32)).astype(jnp.bfloat16)
    weight_grads = (edge_in_grad, edge_out_grad, node_in_grad, node_out_grad)
    device_count = lax.axis_size("nodes") * lax.axis_size("rep")
    edge_scale = 1.0 / math.sqrt(senders.shape[0] * device_count)
    node_scale = 1.0 / math.sqrt(node_latent.shape[0] * device_count)
    weight_total = lax.psum(
        (weight_grads[0], weight_grads[1], weight_grads[2], weight_grads[3]), ("nodes", "rep")
    )
    return (
        grad_nodes,
        edge_grad,
        (weight_total[0] * edge_scale).astype(jnp.bfloat16),
        (weight_total[1] * edge_scale).astype(jnp.bfloat16),
        (weight_total[2] * node_scale).astype(jnp.bfloat16),
        (weight_total[3] * node_scale).astype(jnp.bfloat16),
    )


def solution(mesh):
    return jax.shard_map(
        shards,
        mesh=mesh,
        in_specs=(
            P(("nodes", "rep"), None),
            P(("nodes", "rep"), None),
            P(("nodes", "rep"), None),
            P(("nodes", "rep"), None),
            P(("nodes", "rep")),
            P(("nodes", "rep")),
            P("nodes", None, None),
            P(),
            P(),
            P(),
            P(),
            P(),
            P(),
            P(),
        ),
        out_specs=(P(("nodes", "rep"), None), P(("nodes", "rep"), None), P(), P(), P(), P()),
        check_vma=False,
    )
```

profile of v0, /device:TPU:0, one launch (start us, length us, event | category | flops | bytes accessed | tf_op | source)
XLA Modules:
  0.0 329.2 jit_solution(6399339282677917739)
XLA Ops:
  7.2 2.5 all_gather.6
  10.6 1.5 gather_fusion
  12.1 8.2 %all-to-all-start = ((bf16[16,8,512]{2,1,0:T(8,128)(2,1)}), bf16[16,8,512]{2,1,0:T(8,128)(2,1)S(1)}, u32[]{:S(2)}, u32[]{:S(2)}) async-start(bf16[16,8,512]{2,1,0:T(8,128)(2,1)} %bitcast.1), calls=%async_computation | async-start | bytes 262144 | tf_op jit(solution)/shard_map/all_to_all | solution.py:132
  21.1 4.1 %gather_fusion.2 = bf16[1280,512]{1,0:T(8,128)(2,1)S(1)} fusion(bf16[320,512]{1,0:T(8,128)(2,1)S(1)} %all_gather.6, s32[2048]{0:T(1024)S(1)} %pad_clamp_fusion), kind=kCustom, calls=%fused_computation.2 | custom fusion | bytes 2626560 | tf_op jit(solution)/shard_map/gather | solution.py:137
  25.3 3.8 %fusion.15 = f32[1280,512]{1,0:T(8,128)} fusion(bf16[1280,512]{1,0:T(8,128)(2,1)S(1)} %gather_fusion.2, bf16[1536,512]{1,0:T(8,128)(2,1)} %param.21), kind=kOutput, calls=%fused_computation.46 | convolution fusion | flops 671088640 | bytes 4456448 | tf_op jit(solution)/shard_map/dot_general | solution.py:15
  29.1 4.1 %gather_fusion.1 = bf16[1280,512]{1,0:T(8,128)(2,1)S(1)} fusion(bf16[448,512]{1,0:T(8,128)(2,1)S(1)} %pad_maximum_fusion.2, s32[2048]{0:T(1024)S(1)} %pad_clamp_fusion.1), kind=kCustom, calls=%fused_computation.1 | custom fusion | bytes 2626560 | tf_op jit(solution)/shard_map/gather | solution.py:136
  33.2 2.4 fusion.19
  35.7 4.2 %multiply_convert_fusion.2 = (bf16[1280,512]{1,0:T(8,128)(2,1)S(1)}, f32[1280,512]{1,0:T(8,128)}) fusion(f32[1280,512]{1,0:T(8,128)S(1)} %copy-done.12, f32[1280,512]{1,0:T(8,128)S(1)} %fusion.19, bf16[1280,512]{1,0:T(8,128)(2,1)} %collective-permute-done, bf16[1536,512]{1,0:T(8,128)(2,1)} %param.21), kind=kOutput, calls=%fused_computation.22 | convolution fusion | flops 675676160 | bytes 11010048 | tf_op jit(solution)/shard_map/dot_general | solution.py:15
  39.9 0.9 fusion.47
  41.7 1.9 multiply_add_fusion
  43.6 3.2 copy.28
  46.9 11.1 %scatter_custom_fusion = f32[320,512]{1,0:T(8,128)} fusion(s32[1280]{0:T(1024)S(1)} %copy-done.34, f32[1280,512]{1,0:T(8,128)} %copy.28, f32[]{:T(128)} %constant.10.clone.1), kind=kCustom, calls=%fused_computation.70 | custom fusion | flops 655360 | bytes 655872 | tf_op jit(solution)/shard_map/scatter-add | solution.py:141
  58.1 2.4 copy.27
  60.5 2.0 fusion.11
  62.5 5.1 %reduce-scatter.3.cloned.1.call-done = f32[160,512]{1,0:T(8,128)} async-done(((f32[320,512]{1,0:T(8,128)}), f32[160,512]{1,0:T(8,128)}) %reduce-scatter.3.cloned.1.call-update) | async-done | bytes 327696 | tf_op jit(solution)/shard_map/reduce_scatter | solution.py:142
  67.6 1.5 convolution_add_fusion.3
  69.2 1.5 fusion.48
  72.7 2.2 all_gather.7
  74.9 4.7 %gather_fusion.3 = bf16[1280,512]{1,0:T(8,128)(2,1)} fusion(bf16[320,512]{1,0:T(8,128)(2,1)S(1)} %all_gather.7, s32[2048]{0:T(1024)S(1)} %pad_clamp_fusion), kind=kCustom, calls=%fused_computation.3 | custom fusion | bytes 2626560 | tf_op jit(solution)/shard_map/gather | solution.py:147
  79.6 2.4 copy.29
  82.1 2.7 fusion.4
  84.8 1.0 multiply_convert_fusion.1
  86.5 1.5 fusion.2
  88.0 2.4 fusion.17
  90.5 2.4 fusion.13
  92.8 10.6 %scatter_custom_fusion.1 = f32[448,512]{1,0:T(8,128)S(1)} fusion(s32[1280]{0:T(1024)S(1)} %copy-done.36, f32[1280,512]{1,0:T(8,128)} %fusion.17, f32[]{:T(128)} %constant.10.clone.1), kind=kCustom, calls=%fused_computation.55 | custom fusion | flops 655360 | bytes 918016 | tf_op jit(solution)/shard_map/scatter-add | solution.py:161
  104.1 3.2 fusion.50
  107.4 1.4 fusion.43
  108.8 6.7 %all-to-all-start.1 = ((bf16[16,8,512]{2,1,0:T(8,128)(2,1)}), bf16[16,8,512]{2,1,0:T(8,128)(2,1)S(1)}, u32[]{:S(2)}, u32[]{:S(2)}) async-start(bf16[16,8,512]{2,1,0:T(8,128)(2,1)} %fusion.37), calls=%async_computation.2 | async-start | bytes 262144 | tf_op jit(solution)/shard_map/all_to_all | solution.py:166
  115.7 10.7 %scatter_fusion = f32[320,512]{1,0:T(8,128)S(1)} fusion(f32[320,512]{1,0:T(8,128)S(1)} %slice.42, s32[1280]{0:T(1024)S(1)} %copy-done.34, f32[1280,512]{1,0:T(8,128)} %fusion.13), kind=kCustom, calls=%fused_computation.6 | custom fusion | flops 655360 | bytes 7869440 | tf_op jit(solution)/shard_map/scatter-add | solution.py:162
  126.4 1.3 fusion.39
  127.8 1.3 convolution_bitcast_fusion.1
  129.1 1.5 scatter_custom_fusion.3
  130.6 1.0 add.134
  131.7 3.2 pad_maximum_fusion.1
  134.9 0.9 fusion.49
  136.6 1.9 fusion.51
  138.5 2.3 convolution_bitcast_fusion
  140.8 2.0 pad_maximum_fusion
  142.9 1.3 copy-done.3
  144.1 3.0 fusion.1
  147.1 2.5 copy.32
  149.6 2.0 fusion.7
  151.6 164.3 %all-reduce.3.cloned.1.call-done = (f32[1536,512]{1,0:T(8,128)}, f32[512,512]{1,0:T(8,128)}, f32[1024,512]{1,0:T(8,128)}, f32[512,512]{1,0:T(8,128)}) async-done(((f32[1536,512]{1,0:T(8,128)}, f32[512,512]{1,0:T(8,128)}, f32[1024,512]{1,0:T(8,128)}, f32[512,512]{1,0:T(8,128)}), (f32[1536,512]{1,0:T(8,128)}, f32[512,512]{1,0:T(8,128)}, f32[1024,512]{1,0:T(8,128)}, ...) | async-done | bytes 7340048 | tf_op jit(solution)/shard_map/psum | solution.py:178
  315.9 3.6 %multiply_convert_fusion = bf16[1536,512]{1,0:T(8,128)(2,1)} fusion(f32[1536,512]{1,0:T(8,128)} %get-tuple-element.22), kind=kLoop, calls=%fused_computation.14 | loop fusion | flops 1572864 | bytes 4718592 | tf_op jit(solution)/shard_map/convert_element_type | solution.py:184
  319.5 0.9 multiply_convert_fusion.5
  320.4 1.3 multiply_convert_fusion.3
  321.7 0.9 multiply_convert_fusion.4
  (116 shorter events, 7.2 us)
Async XLA Ops:
  7.2 32.7 %copy-start = (bf16[512,512]{1,0:T(8,128)(2,1)S(1)}, bf16[512,512]{1,0:T(8,128)(2,1)}, u32[]{:S(2)}) copy-start(bf16[512,512]{1,0:T(8,128)(2,1)} %param.22) | copy-start | bytes 1572868
  12.1 17.0 %all-to-all-start = ((bf16[16,8,512]{2,1,0:T(8,128)(2,1)}), bf16[16,8,512]{2,1,0:T(8,128)(2,1)S(1)}, u32[]{:S(2)}, u32[]{:S(2)}) async-start(bf16[16,8,512]{2,1,0:T(8,128)(2,1)} %bitcast.1), calls=%async_computation | async-start | bytes 262144 | tf_op jit(solution)/shard_map/all_to_all | solution.py:132
  20.3 47.3 %reduce-scatter.3.cloned.1.call-start = ((), (), s32[]{:S(2)}) async-start(), calls=%async_computation.4 | async-start | bytes 983040 | tf_op jit(solution)/shard_map/reduce_scatter | solution.py:142
  20.3 15.3 %collective-permute-start = (bf16[1280,512]{1,0:T(8,128)(2,1)}, bf16[1280,512]{1,0:T(8,128)(2,1)}, u32[]{:S(2)}, u32[]{:S(2)}) collective-permute-start(bf16[1280,512]{1,0:T(8,128)(2,1)} %param.15), channel_id=1, source_target_pairs={{0,1},{1,0},{2,3},{3,2},{4,5},{5,4},{6,7},{7,6},{8,9},{9,8},{10,11... | collective-permute-start | bytes 3932168 | tf_op jit(solution)/shard_map/ppermute | solution.py:11
  21.1 4.1 %copy-start.36 = (s32[1280]{0:T(1024)S(1)}, s32[1280]{0:T(1024)}, u32[]{:S(2)}) copy-start(s32[1280]{0:T(1024)} %param.18) | copy-start | bytes 15364
  25.3 3.8 %copy-start.7 = (bf16[1280,512]{1,0:T(8,128)(2,1)}, bf16[1280,512]{1,0:T(8,128)(2,1)S(1)}, u32[]{:S(2)}) copy-start(bf16[1280,512]{1,0:T(8,128)(2,1)S(1)} %gather_fusion.2) | copy-start | bytes 3932164
  33.2 2.4 copy-start.5
  33.2 2.4 copy-start.12
  39.9 1.1 copy-start.22
  41.0 0.7 copy-start.35
  41.0 0.7 copy-start.37
  43.6 3.2 copy-start.34
  46.8 13.6 %copy-start.16 = (bf16[160,512]{1,0:T(8,128)(2,1)S(1)}, bf16[160,512]{1,0:T(8,128)(2,1)}, u32[]{:S(2)}) copy-start(bf16[160,512]{1,0:T(8,128)(2,1)} %param.14) | copy-start | bytes 491524
  62.5 8.4 %copy-start.30 = (bf16[160,512]{1,0:T(8,128)(2,1)S(1)}, bf16[160,512]{1,0:T(8,128)(2,1)}, u32[]{:S(2)}) copy-start(bf16[160,512]{1,0:T(8,128)(2,1)} %param.16) | copy-start | bytes 491524
  62.5 8.4 %copy-start.38 = (f32[512]{0:T(512)S(1)}, f32[512]{0:T(512)}, u32[]{:S(2)}) copy-start(f32[512]{0:T(512)} %param.27) | copy-start | bytes 6148
  67.6 3.6 %copy-start.39 = (bf16[512,512]{1,0:T(8,128)(2,1)S(1)}, bf16[512,512]{1,0:T(8,128)(2,1)}, u32[]{:S(2)}) copy-start(bf16[512,512]{1,0:T(8,128)(2,1)} %param.26) | copy-start | bytes 1572868
  69.1 2.4 copy-start.32
  70.7 1.7 copy-start.20
  70.7 1.3 copy-start.13
  72.0 0.7 copy-start.18
  82.0 2.7 copy-start.2
  82.0 2.7 copy-start.4
  84.8 1.7 copy-start.40
  85.8 2.3 copy-start.24
  86.5 1.5 copy-start.11
  88.0 2.4 copy-start.9
  92.8 11.3 %copy-start.8 = (bf16[1280,512]{1,0:T(8,128)(2,1)S(1)}, bf16[1280,512]{1,0:T(8,128)(2,1)}, u32[]{:S(2)}) copy-start(bf16[1280,512]{1,0:T(8,128)(2,1)} %copy-done.7) | copy-start | bytes 3932164
  104.1 3.2 copy-start.21
  104.1 3.2 copy-start.31
  104.1 3.2 copy-start.33
  108.8 20.3 %all-to-all-start.1 = ((bf16[16,8,512]{2,1,0:T(8,128)(2,1)}), bf16[16,8,512]{2,1,0:T(8,128)(2,1)S(1)}, u32[]{:S(2)}, u32[]{:S(2)}) async-start(bf16[16,8,512]{2,1,0:T(8,128)(2,1)} %fusion.37), calls=%async_computation.2 | async-start | bytes 262144 | tf_op jit(solution)/shard_map/all_to_all | solution.py:166
  115.6 10.8 %copy-start.19 = (bf16[160,512]{1,0:T(8,128)(2,1)S(1)}, bf16[160,512]{1,0:T(8,128)(2,1)}, u32[]{:S(2)}) copy-start(bf16[160,512]{1,0:T(8,128)(2,1)} %copy-done.18) | copy-start | bytes 491524
  115.6 10.8 %copy-start.26 = (f32[160,512]{1,0:T(8,128)S(1)}, f32[160,512]{1,0:T(8,128)}, u32[]{:S(2)}) copy-start(f32[160,512]{1,0:T(8,128)} %reduce-scatter.3.cloned.1.call-done) | copy-start | bytes 983044
  115.6 12.2 %copy-start.17 = (bf16[160,512]{1,0:T(8,128)(2,1)S(1)}, bf16[160,512]{1,0:T(8,128)(2,1)}, u32[]{:S(2)}) copy-start(bf16[160,512]{1,0:T(8,128)(2,1)} %param.14) | copy-start | bytes 491524
  115.6 34.0 %reduce-scatter.5.cloned.1.call-start = ((), (), s32[]{:S(2)}) async-start(), calls=%async_computation.5 | async-start | bytes 983040 | tf_op jit(solution)/shard_map/reduce_scatter | solution.py:172
  131.6 3.3 %copy-start.6 = (bf16[1280,512]{1,0:T(8,128)(2,1)S(1)}, bf16[1280,512]{1,0:T(8,128)(2,1)}, u32[]{:S(2)}) copy-start(bf16[1280,512]{1,0:T(8,128)(2,1)} %copy-done.5) | copy-start | bytes 3932164
  131.6 3.3 copy-start.10
  131.6 184.3 %all-reduce.3.cloned.1.call-start = ((), (), s32[]{:S(2)}) async-start(), calls=%async_computation.6 | async-start | bytes 14680064 | tf_op jit(solution)/shard_map/psum | solution.py:178
  134.9 1.3 copy-start.23
  134.9 1.7 copy-start.25
  138.5 2.3 copy-start.29
  142.8 1.3 copy-start.3
  147.1 2.5 copy-start.14
  315.9 3.6 %copy-start.28 = (f32[512,512]{1,0:T(8,128)S(1)}, f32[512,512]{1,0:T(8,128)}, u32[]{:S(2)}) copy-start(f32[512,512]{1,0:T(8,128)} %get-tuple-element.23) | copy-start | bytes 3145732
  315.9 4.6 %copy-start.15 = (f32[1024,512]{1,0:T(8,128)S(1)}, f32[1024,512]{1,0:T(8,128)}, u32[]{:S(2)}) copy-start(f32[1024,512]{1,0:T(8,128)} %get-tuple-element.24) | copy-start | bytes 6291460
  319.5 2.2 copy-start.27
  320.4 2.2 copy-start.1
Sparse Core Ops, SparseCore 0:
  58.1 9.4 reduce-scatter.2
  131.7 9.3 reduce-scatter.4
  147.3 168.5 all-reduce.2
where the time goes:
time: 330 us; the launch traced here: 329 us
  waiting for transfers between devices  169 us (51%)
  other arithmetic  53.9 us (16%)
  matrix products  40.7 us (12%)
  local copies, waits for them, and re-layouts  31 us (9%)
  starting transfers between devices  15.1 us (5%)
  between operations  14.3 us (4%)
  blocking collectives  4.72 us (1%)
    psum x1, waiting for transfers between devices, shards(): lax.psum((weight_grads[0], weight_grads[1], weight_grads[2], weight_grads...  164 us
    dot_general x7, matrix products, mat_mul(): return jnp.dot(left, right, preferred_element_type=jnp.float32)  16.4 us
    dot_general x7, matrix products, mat_tn(): lax.dot_general(left, right, (((0,), (0,)), ((), ())), preferred_element_...  12.4 us
    dot_general x7, matrix products, mat_nt(): lax.dot_general(left, right, (((1,), (1,)), ((), ())), preferred_element_...  11.9 us
    scatter-add x1, other arithmetic, shards(): jax.ops.segment_sum(message, receivers, num_segments=part_rows)  11.1 us
    scatter-add x1, other arithmetic, shards(): jax.ops.segment_sum(recv_grad, receivers, num_segments=part_rows)  10.7 us
    scatter-add x1, other arithmetic, shards(): jax.ops.segment_sum(send_grad, senders, num_segments=node_table.shape[0])  10.6 us
    unnamed x85, local copies, waits for them, and re-layouts  10.1 us
  transfers between devices with their start and end apart: 6, of which 2 were waited for; matrix products, arithmetic and copies ran while one was open for 15% of the time, Pallas kernels for 0%

commit v1 on v0

--- a/solution.py
+++ b/solution.py
@@ -176,7 +176,8 @@
     edge_scale = 1.0 / math.sqrt(senders.shape[0] * device_count)
     node_scale = 1.0 / math.sqrt(node_latent.shape[0] * device_count)
     weight_total = lax.psum(
-        (weight_grads[0], weight_grads[1], weight_grads[2], weight_grads[3]), ("nodes", "rep")
+        lax.psum((weight_grads[0], weight_grads[1], weight_grads[2], weight_grads[3]), "rep"),
+        "nodes",
     )
     return (
         grad_nodes,

time: 330 us -> 406 us (1.23)
  waiting for transfers between devices: 169 us -> 246 us
    psum x0 -> x1, waiting for transfers between devices: none -> 238 us  [shards(): lax.psum(lax.psum((weight_grads[0], weight_grads[1], weight_grads[2], wei...]
    psum x1, waiting for transfers between devices: 164 us -> 0.02 us  [shards(): lax.psum((weight_grads[0], weight_grads[1], weight_grads[2], weight_grads...]
    dot_general x7, matrix products: 12.4 us -> 7.91 us  [mat_tn(): lax.dot_general(left, right, (((0,), (0,)), ((), ())), preferred_element_...]
    unnamed x85 -> x73, local copies, waits for them, and re-layouts: 10.1 us -> 9.69 us
  transfers between devices with their start and end apart: 6 -> 7, of which waited for: 2 -> 3; matrix products, arithmetic and copies ran while one was open for 15% -> 15% of each run, Pallas kernels for 0% -> 0%
where the time goes in v1:
time: 406 us; the launch traced here: 404 us
  waiting for transfers between devices  246 us (61%)
  other arithmetic  53 us (13%)
  matrix products  38.3 us (9%)
  local copies, waits for them, and re-layouts  32.8 us (8%)
  starting transfers between devices  15.2 us (4%)
  between operations  14.2 us (3%)
  blocking collectives  4.72 us (1%)
    psum x1, waiting for transfers between devices, shards(): lax.psum(lax.psum((weight_grads[0], weight_grads[1], weight_grads[2], wei...  238 us
    dot_general x7, matrix products, mat_mul(): return jnp.dot(left, right, preferred_element_type=jnp.float32)  16.4 us
    dot_general x7, matrix products, mat_nt(): lax.dot_general(left, right, (((1,), (1,)), ((), ())), preferred_element_...  14 us
    scatter-add x1, other arithmetic, shards(): jax.ops.segment_sum(send_grad, senders, num_segments=node_table.shape[0])  11.4 us
    scatter-add x1, other arithmetic, shards(): jax.ops.segment_sum(message, receivers, num_segments=part_rows)  11.1 us
    scatter-add x1, other arithmetic, shards(): jax.ops.segment_sum(recv_grad, receivers, num_segments=part_rows)  10.6 us
    unnamed x73, local copies, waits for them, and re-layouts  9.69 us
    all_to_all x1, starting transfers between devices, shards(): lax.all_to_all(outgoing, 'nodes', split_axis=0, concat_axis=0, tiled=True)  8.22 us
  transfers between devices with their start and end apart: 7, of which 3 were waited for; matrix products, arithmetic and copies ran while one was open for 15% of the time, Pallas kernels for 0%

profile of v1, /device:TPU:0, one launch (start us, length us, event | category | flops | bytes accessed | tf_op | source)
XLA Modules:
  0.0 404.4 jit_solution(8770099151280090882)
XLA Ops:
  7.2 2.5 all_gather.6
  10.6 1.5 gather_fusion
  12.1 8.2 %all-to-all-start = ((bf16[16,8,512]{2,1,0:T(8,128)(2,1)}), bf16[16,8,512]{2,1,0:T(8,128)(2,1)S(1)}, u32[]{:S(2)}, u32[]{:S(2)}) async-start(bf16[16,8,512]{2,1,0:T(8,128)(2,1)} %bitcast.1), calls=%async_computation | async-start | bytes 262144 | tf_op jit(solution)/shard_map/all_to_all | solution.py:132
  21.1 4.1 %gather_fusion.2 = bf16[1280,512]{1,0:T(8,128)(2,1)S(1)} fusion(bf16[320,512]{1,0:T(8,128)(2,1)S(1)} %all_gather.6, s32[2048]{0:T(1024)S(1)} %pad_clamp_fusion), kind=kCustom, calls=%fused_computation.2 | custom fusion | bytes 2626560 | tf_op jit(solution)/shard_map/gather | solution.py:137
  25.3 3.7 fusion.15
  29.1 4.1 %gather_fusion.1 = bf16[1280,512]{1,0:T(8,128)(2,1)S(1)} fusion(bf16[448,512]{1,0:T(8,128)(2,1)S(1)} %pad_maximum_fusion.2, s32[2048]{0:T(1024)S(1)} %pad_clamp_fusion.1), kind=kCustom, calls=%fused_computation.1 | custom fusion | bytes 2626560 | tf_op jit(solution)/shard_map/gather | solution.py:136
  33.2 2.4 fusion.19
  35.6 4.3 %multiply_convert_fusion.2 = (bf16[1280,512]{1,0:T(8,128)(2,1)S(1)}, f32[1280,512]{1,0:T(8,128)}) fusion(f32[1280,512]{1,0:T(8,128)S(1)} %copy-done.9, f32[1280,512]{1,0:T(8,128)S(1)} %fusion.19, bf16[1280,512]{1,0:T(8,128)(2,1)} %collective-permute-done, bf16[1536,512]{1,0:T(8,128)(2,1)} %param.21), kind=kOutput, calls=%fused_computation.22 | convolution fusion | flops 675676160 | bytes 11010048 | tf_op jit(solution)/shard_map/dot_general | solution.py:15
  39.9 0.9 fusion.47
  41.7 1.9 multiply_add_fusion
  43.6 3.3 copy.28
  47.0 11.1 %scatter_custom_fusion = f32[320,512]{1,0:T(8,128)} fusion(s32[1280]{0:T(1024)S(1)} %copy-done.28, f32[1280,512]{1,0:T(8,128)} %copy.28, f32[]{:T(128)} %constant.10.clone.1), kind=kCustom, calls=%fused_computation.70 | custom fusion | flops 655360 | bytes 655872 | tf_op jit(solution)/shard_map/scatter-add | solution.py:141
  58.1 2.4 copy.27
  60.6 2.0 fusion.11
  62.6 5.1 %reduce-scatter.3.cloned.1.call-done = f32[160,512]{1,0:T(8,128)} async-done(((f32[320,512]{1,0:T(8,128)}), f32[160,512]{1,0:T(8,128)}) %reduce-scatter.3.cloned.1.call-update) | async-done | bytes 327696 | tf_op jit(solution)/shard_map/reduce_scatter | solution.py:142
  67.7 1.5 convolution_add_fusion.3
  69.3 1.5 fusion.48
  72.8 2.2 all_gather.7
  75.0 4.7 %gather_fusion.3 = bf16[1280,512]{1,0:T(8,128)(2,1)} fusion(bf16[320,512]{1,0:T(8,128)(2,1)S(1)} %all_gather.7, s32[2048]{0:T(1024)S(1)} %pad_clamp_fusion), kind=kCustom, calls=%fused_computation.3 | custom fusion | bytes 2626560 | tf_op jit(solution)/shard_map/gather | solution.py:147
  79.7 2.4 copy.29
  82.2 2.7 fusion.4
  84.9 1.0 multiply_convert_fusion.1
  86.6 1.5 fusion.2
  88.1 0.9 fusion.50
  89.5 0.9 fusion.49
  90.8 1.9 fusion.51
  93.0 1.4 fusion.43
  94.8 1.6 pad_maximum_fusion.1
  96.4 2.2 convolution_bitcast_fusion
  98.6 2.1 pad_maximum_fusion
  100.7 3.4 fusion.17
  104.2 11.4 %scatter_custom_fusion.1 = f32[448,512]{1,0:T(8,128)} fusion(s32[1280]{0:T(1024)S(1)} %copy-done.30, f32[1280,512]{1,0:T(8,128)} %fusion.17, f32[]{:T(128)} %constant.10.clone.1), kind=kCustom, calls=%fused_computation.55 | custom fusion | flops 655360 | bytes 918016 | tf_op jit(solution)/shard_map/scatter-add | solution.py:161
  115.6 1.2 slice.42
  116.7 1.6 fusion.37
  118.4 6.7 %all-to-all-start.1 = ((bf16[16,8,512]{2,1,0:T(8,128)(2,1)}), bf16[16,8,512]{2,1,0:T(8,128)(2,1)S(1)}, u32[]{:S(2)}, u32[]{:S(2)}) async-start(bf16[16,8,512]{2,1,0:T(8,128)(2,1)} %fusion.37), calls=%async_computation.2 | async-start | bytes 262144 | tf_op jit(solution)/shard_map/all_to_all | solution.py:166
  125.2 3.5 fusion.13
  128.6 10.6 %scatter_fusion = f32[320,512]{1,0:T(8,128)S(1)} fusion(f32[320,512]{1,0:T(8,128)S(1)} %slice.42, s32[1280]{0:T(1024)S(1)} %copy-done.28, f32[1280,512]{1,0:T(8,128)} %fusion.13), kind=kCustom, calls=%fused_computation.6 | custom fusion | flops 655360 | bytes 7869440 | tf_op jit(solution)/shard_map/scatter-add | solution.py:162
  139.3 1.5 scatter_custom_fusion.3
  140.8 1.0 add.142
  143.2 3.0 fusion.1
  146.1 2.5 copy.32
  148.7 2.6 reduce-scatter.5.cloned.1.call-done
  151.3 2.0 fusion.7
  153.2 237.9 %all-reduce.5.cloned.1.call-done = (f32[1536,512]{1,0:T(8,128)}, f32[512,512]{1,0:T(8,128)}, f32[1024,512]{1,0:T(8,128)}, f32[512,512]{1,0:T(8,128)}) async-done(((f32[1536,512]{1,0:T(8,128)}, f32[512,512]{1,0:T(8,128)}, f32[1024,512]{1,0:T(8,128)}, f32[512,512]{1,0:T(8,128)}), (f32[1536,512]{1,0:T(8,128)}, f32[512,512]{1,0:T(8,128)}, f32[1024,512]{1,0:T(8,128)}, ...) | async-done | bytes 7340048 | tf_op jit(solution)/shard_map/psum | solution.py:178
  391.1 3.6 multiply_convert_fusion
  394.8 0.9 multiply_convert_fusion.5
  395.7 1.3 multiply_convert_fusion.3
  396.9 0.9 multiply_convert_fusion.4
  (107 shorter events, 8.6 us)
Async XLA Ops:
  7.2 32.8 %copy-start = (bf16[512,512]{1,0:T(8,128)(2,1)S(1)}, bf16[512,512]{1,0:T(8,128)(2,1)}, u32[]{:S(2)}) copy-start(bf16[512,512]{1,0:T(8,128)(2,1)} %param.22) | copy-start | bytes 1572868
  12.1 17.0 %all-to-all-start = ((bf16[16,8,512]{2,1,0:T(8,128)(2,1)}), bf16[16,8,512]{2,1,0:T(8,128)(2,1)S(1)}, u32[]{:S(2)}, u32[]{:S(2)}) async-start(bf16[16,8,512]{2,1,0:T(8,128)(2,1)} %bitcast.1), calls=%async_computation | async-start | bytes 262144 | tf_op jit(solution)/shard_map/all_to_all | solution.py:132
  20.3 47.4 %reduce-scatter.3.cloned.1.call-start = ((), (), s32[]{:S(2)}) async-start(), calls=%async_computation.4 | async-start | bytes 983040 | tf_op jit(solution)/shard_map/reduce_scatter | solution.py:142
  20.3 15.3 %collective-permute-start = (bf16[1280,512]{1,0:T(8,128)(2,1)}, bf16[1280,512]{1,0:T(8,128)(2,1)}, u32[]{:S(2)}, u32[]{:S(2)}) collective-permute-start(bf16[1280,512]{1,0:T(8,128)(2,1)} %param.15), channel_id=1, source_target_pairs={{0,1},{1,0},{2,3},{3,2},{4,5},{5,4},{6,7},{7,6},{8,9},{9,8},{10,11... | collective-permute-start | bytes 3932168 | tf_op jit(solution)/shard_map/ppermute | solution.py:11
  21.1 4.1 %copy-start.30 = (s32[1280]{0:T(1024)S(1)}, s32[1280]{0:T(1024)}, u32[]{:S(2)}) copy-start(s32[1280]{0:T(1024)} %param.18) | copy-start | bytes 15364
  25.3 3.8 copy-start.5
  33.2 2.4 copy-start.7
  33.2 2.4 copy-start.9
  39.9 1.1 copy-start.19
  41.0 0.7 copy-start.29
  41.0 0.7 copy-start.31
  43.6 3.3 copy-start.28
  47.0 13.6 %copy-start.13 = (bf16[160,512]{1,0:T(8,128)(2,1)S(1)}, bf16[160,512]{1,0:T(8,128)(2,1)}, u32[]{:S(2)}) copy-start(bf16[160,512]{1,0:T(8,128)(2,1)} %param.14) | copy-start | bytes 491524
  58.1 83.8 %all-reduce.7.cloned.1.call-start = ((), (), s32[]{:S(2)}) async-start(), calls=%async_computation.7 | async-start | bytes 14680064 | tf_op jit(solution)/shard_map/psum | solution.py:179
  62.6 8.4 %copy-start.24 = (bf16[160,512]{1,0:T(8,128)(2,1)S(1)}, bf16[160,512]{1,0:T(8,128)(2,1)}, u32[]{:S(2)}) copy-start(bf16[160,512]{1,0:T(8,128)(2,1)} %param.16) | copy-start | bytes 491524
  62.6 8.4 %copy-start.32 = (f32[512]{0:T(512)S(1)}, f32[512]{0:T(512)}, u32[]{:S(2)}) copy-start(f32[512]{0:T(512)} %param.27) | copy-start | bytes 6148
  67.7 3.6 copy-start.33
  69.2 2.4 copy-start.26
  70.8 1.7 copy-start.17
  70.8 1.3 copy-start.10
  72.1 0.7 copy-start.15
  82.2 2.7 copy-start.2
  82.2 2.7 copy-start.4
  84.9 1.7 copy-start.34
  86.6 1.5 copy-start.6
  88.1 1.3 copy-start.8
  89.4 1.3 copy-start.20
  90.8 1.9 copy-start.14
  90.8 1.9 copy-start.16
  90.8 2.3 copy-start.18
  90.8 2.3 copy-start.25
  90.8 2.3 copy-start.27
  92.7 1.8 copy-start.21
  118.4 20.9 %all-to-all-start.1 = ((bf16[16,8,512]{2,1,0:T(8,128)(2,1)}), bf16[16,8,512]{2,1,0:T(8,128)(2,1)S(1)}, u32[]{:S(2)}, u32[]{:S(2)}) async-start(bf16[16,8,512]{2,1,0:T(8,128)(2,1)} %fusion.37), calls=%async_computation.2 | async-start | bytes 262144 | tf_op jit(solution)/shard_map/all_to_all | solution.py:166
  125.1 26.1 %reduce-scatter.5.cloned.1.call-start = ((), (), s32[]{:S(2)}) async-start(), calls=%async_computation.5 | async-start | bytes 983040 | tf_op jit(solution)/shard_map/reduce_scatter | solution.py:172
  141.8 249.4 %all-reduce.5.cloned.1.call-start = ((), (), s32[]{:S(2)}) async-start(), calls=%async_computation.6 | async-start | bytes 14680064 | tf_op jit(solution)/shard_map/psum | solution.py:178
  141.8 1.3 copy-start.3
  146.1 5.1 %copy-start.11 = (bf16[1024,512]{1,0:T(8,128)(2,1)S(1)}, bf16[1024,512]{1,0:T(8,128)(2,1)}, u32[]{:S(2)}) copy-start(bf16[1024,512]{1,0:T(8,128)(2,1)} %param.25) | copy-start | bytes 3145732
  391.1 3.6 copy-start.23
  391.1 4.6 %copy-start.12 = (f32[1024,512]{1,0:T(8,128)S(1)}, f32[1024,512]{1,0:T(8,128)}, u32[]{:S(2)}) copy-start(f32[1024,512]{1,0:T(8,128)} %get-tuple-element.24) | copy-start | bytes 6291460
  394.7 2.2 copy-start.22
  395.7 2.2 copy-start.1
Sparse Core Ops, SparseCore 0:
  58.2 9.4 reduce-scatter.2
  100.8 35.5 all-reduce.6
  141.9 9.3 reduce-scatter.4
  157.5 233.5 all-reduce.4
